TPU v7x, 128 devices: a whole 4x4x4 slice. The times are simulated.
128 devices in a mesh: sector: 16 (over x, z_lo, core), slab: 8 (over y, z_hi).
Axes of the slice: x: 4, y: 4, z: 4 (z_hi: 2, z_lo: 2; z = z_hi * 2 + z_lo), core: 2. Of those that a mesh axis runs over, the one named last changes fastest.
Arguments:
- right_basis: float32 [64, 128, 96, 256], P(None, 'sector', 'slab')
- left_basis: float32 [64, 128, 96, 256], P(None, 'sector', 'slab')
- speed_squared: float32 [128, 96, 256], P('sector', 'slab'), may hold values from 0.5 to 8
- rayleigh: float32 [64, 64], replicated
- schur_order: int32 [64], replicated, may hold values from 0 to 63, each once
- kept_index: int32 [32], replicated, may hold values from 0 to 63, as said below
- rim_map: int32 [256], replicated, may hold values from 0 to 255, each once
Outputs:
- new_right: float32 [32, 128, 96, 256], P(None, 'sector', 'slab')
- new_left: float32 [32, 128, 96, 256], P(None, 'sector', 'slab')
- right_image: float32 [32, 128, 96, 256], P(None, 'sector', 'slab')
- left_image: float32 [32, 128, 96, 256], P(None, 'sector', 'slab')
- restarted: float32 [32, 32], replicated
Inputs may be any that keep to these rules, and one draw needn't show every extreme that they name: `kept_index`: 32 distinct basis indices, 0 and 63 among them. `schur_order`: each basis index once. `rim_map`: each radial cell once.
All inputs are finite; a program needn't handle non-finite values.
Results may differ from a plain program's by a relative error of at most 0.0003.
Values sent between devices are 32-bit elements; how exact they have to be, the bound alone decides.
A program may use at most 256 MiB of HBM per device.

v0:
```python
import jax
import jax.numpy as jnp
from jax import lax
from jax.sharding import PartitionSpec as P


def padded_2(shard, sides, width, wrap):
    for axis, dim in sides:
        peers, length = (lax.axis_size(axis), shard.shape[dim])
        up = [(i, (i + 1) % peers) for i in range(peers if wrap else peers - 1)]
        down = [(j, i) for i, j in up]
        last = lax.slice_in_dim(shard, length - width, length, axis=dim)
        first = lax.slice_in_dim(shard, 0, width, axis=dim)
        before = lax.ppermute(last, axis, up)
        after = lax.ppermute(first, axis, down)
        shard = jnp.concatenate([before, shard, after], axis=dim)
    return shard


def exact_dot(left_operator, right_operator):
    return jnp.dot(left_operator, right_operator, precision=lax.Precision.HIGHEST)


def lower_inverse(lower_factor):
    identity = jnp.eye(lower_factor.shape[0], dtype=lower_factor.dtype)
    return lax.linalg.triangular_solve(lower_factor, identity, left_side=True, lower=True)


def solve_inverse(cross_matrix):
    normal_matrix = exact_dot(cross_matrix.T, cross_matrix)
    scaling_factor = jnp.linalg.cholesky(normal_matrix)
    middle = lax.linalg.triangular_solve(scaling_factor, cross_matrix.T, left_side=True, lower=True)
    return lax.linalg.triangular_solve(
        scaling_factor, middle, left_side=True, lower=True, transpose_a=True
    )


def orthonormal(matrix):

    def column_step(column_index, partial_basis):
        column_index = jnp.asarray(column_index).astype(jnp.int32)
        column = lax.dynamic_slice_in_dim(matrix, column_index, 1, 1)
        column = column - exact_dot(partial_basis, exact_dot(partial_basis.T, column))
        column = column - exact_dot(partial_basis, exact_dot(partial_basis.T, column))
        column = column / jnp.sqrt(jnp.sum(column * column))
        return lax.dynamic_update_slice_in_dim(partial_basis, column, column_index, 1)

    return lax.fori_loop(0, matrix.shape[1], column_step, jnp.zeros_like(matrix))


def select_matrix(chosen, total):
    return (jnp.arange(total)[:, None] == chosen[None, :]).astype(jnp.float32)


def small_step(lower_factor, lower_inverse_mat, cross_inverse, rayleigh, schur_order, kept_index):
    total = rayleigh.shape[0]
    turned = exact_dot(exact_dot(lower_factor.T, rayleigh), lower_inverse_mat.T)
    select_order = select_matrix(schur_order, total)
    permuted = exact_dot(exact_dot(select_order.T, turned), select_order)
    orthogonal = orthonormal(permuted)
    kept_basis = exact_dot(orthogonal, select_matrix(kept_index, total))
    restarted = exact_dot(exact_dot(kept_basis.T, permuted), kept_basis)
    return (
        restarted,
        exact_dot(kept_basis.T, lower_inverse_mat),
        exact_dot(kept_basis.T, cross_inverse),
    )


def laplace(vector_columns, rim_map, inverse_map):
    wrapped = padded_2(vector_columns, (("sector", 1),), 1, True)
    lower_rim = jnp.take(wrapped[:, 0], inverse_map, axis=2)
    upper_rim = jnp.take(wrapped[:, -1], rim_map, axis=2)
    forward = jnp.concatenate([vector_columns[:, 1:], upper_rim[:, None]], axis=1)
    behind = jnp.concatenate([lower_rim[:, None], vector_columns[:, :-1]], axis=1)
    slab_split = padded_2(vector_columns, (("slab", 2),), 1, False)
    padded = jnp.pad(vector_columns, ((0, 0), (0, 0), (0, 0), (1, 1)))
    final_result = 6.0 * vector_columns - forward - behind
    final_result = final_result - slab_split[:, :, 2:] - slab_split[:, :, :-2]
    return final_result - padded[..., 2:] - padded[..., :-2]


def local(right_basis, left_basis, speed_squared, rayleigh, schur_order, kept_index, rim_map):
    basis_count = right_basis.shape[0]
    kept_count = kept_index.shape[0]
    grid_shape = speed_squared.shape
    right_rows = right_basis.reshape(basis_count, -1)
    left_rows = left_basis.reshape(basis_count, -1)
    flat_speed = speed_squared.reshape(1, -1)
    radial_count = rim_map.shape[0]
    places = jnp.arange(radial_count, dtype=jnp.int32)
    inverse_map = jnp.sum(
        jnp.where(rim_map[:, None] == places[None, :], places[:, None], 0), axis=0
    )
    row_total = right_rows.shape[1] * lax.axis_size("sector") * lax.axis_size("slab")
    right_gram = lax.psum(exact_dot(right_rows, right_rows.T), ("sector", "slab")) / row_total
    lower_factor = jnp.linalg.cholesky(right_gram)
    lower_inverse_mat = lower_inverse(lower_factor)
    normalized = exact_dot(lower_inverse_mat, right_rows)
    cross_matrix = lax.psum(exact_dot(left_rows, normalized.T), ("sector", "slab")) / row_total
    cross_inverse = solve_inverse(cross_matrix)
    restarted, rotate_right, rotate_left = small_step(
        lower_factor, lower_inverse_mat, cross_inverse, rayleigh, schur_order, kept_index
    )
    new_right = exact_dot(rotate_right, right_rows)
    new_left = exact_dot(rotate_left, left_rows)
    stacked = jnp.concatenate([new_right, flat_speed * new_left], axis=0)
    applied = laplace(
        stacked.reshape((2 * kept_count,) + grid_shape), rim_map, inverse_map
    ).reshape(2 * kept_count, -1)
    right_image = flat_speed * applied[:kept_count] - new_right
    left_image = applied[kept_count:] - new_left
    out_shape = (kept_count,) + grid_shape
    return (
        new_right.reshape(out_shape),
        new_left.reshape(out_shape),
        right_image.reshape(out_shape),
        left_image.reshape(out_shape),
        restarted,
    )


def solution(mesh):
    return jax.shard_map(
        local,
        mesh=mesh,
        in_specs=(
            P(None, "sector", "slab", None),
            P(None, "sector", "slab", None),
            P("sector", "slab", None),
            P(),
            P(),
            P(),
            P(),
        ),
        out_specs=(
            P(None, "sector", "slab", None),
            P(None, "sector", "slab", None),
            P(None, "sector", "slab", None),
            P(None, "sector", "slab", None),
            P(),
        ),
        check_vma=False,
    )
```

profile of v0, /device:TPU:24, one launch (start us, length us, event | category | flops | bytes accessed | tf_op | source)
XLA Modules:
  0.0 507.9 jit_solution(3654096387858231448)
XLA Ops:
  0.7 12.4 %fusion.9 = f32[64,64]{0,1:T(8,128)S(1)} fusion(f32[64,8,12,256]{3,1,2,0:T(8,128)} %param.14), kind=kOutput, calls=%fused_computation.28 | convolution fusion | flops 1207959552 | bytes 6307840 | tf_op jit(solution)/shard_map/dot_general | solution.py:21
  13.1 6.1 %copy.67 = f32[64,8,12,256]{3,2,1,0:T(8,128)} copy(f32[64,8,12,256]{3,1,2,0:T(8,128)S(1)} %copy-done.4) | data formatting | bytes 12582912 | tf_op args[0]
  19.2 66.0 %psum.14 = f32[64,64]{0,1:T(8,128)S(1)} all-reduce(f32[64,64]{0,1:T(8,128)S(1)} %fusion.9), channel_id=1, replica_groups=mesh['sector'=16,'slab'=8] {'sector','slab'}, use_global_device_ids=true, to_apply=%region_0.1 | all-reduce | flops 4096 | bytes 32768 | tf_op jit(solution)/shard_map/psum | solution.py:96
  85.2 5.8 %cholesky.44 = f32[64,64]{1,0:T(8,128)S(1)} custom-call(f32[64,64]{1,0:T(8,128)S(1)} %fusion.21), custom_call_target="Cholesky" | custom-call | tf_op jit(solution)/shard_map/jit(cholesky)/cholesky | solution.py:97
  92.4 4.9 custom-call.10
  97.6 6.8 %reshape.80 = f32[64,24576]{1,0:T(8,128)} reshape(f32[64,8,12,256]{3,2,1,0:T(8,128)} %copy.67) | data formatting | bytes 12582912 | tf_op jit(solution)/shard_map/reshape | solution.py:87
  104.4 8.9 %copy.68 = f32[64,8,12,256]{3,2,1,0:T(8,128)} copy(f32[64,8,12,256]{3,1,2,0:T(8,128)} %param.15) | data formatting | bytes 12582912 | tf_op args[1]
  113.2 6.8 %reshape.82 = f32[64,24576]{1,0:T(8,128)} reshape(f32[64,8,12,256]{3,2,1,0:T(8,128)} %copy.68) | data formatting | bytes 12582912 | tf_op jit(solution)/shard_map/reshape | solution.py:88
  120.0 8.1 %fusion.50 = f32[64,24576]{1,0:T(8,128)S(1)} fusion(f32[64,64]{1,0:T(8,128)S(1)} %fusion.19, f32[64,24576]{1,0:T(8,128)} %reshape.80), kind=kOutput, calls=%fused_computation.89 | convolution fusion | flops 1207959552 | bytes 12599296 | tf_op jit(solution)/shard_map/dot_general | solution.py:21
  128.2 5.1 %convolution_bitcast_fusion.4 = f32[64,64]{0,1:T(8,128)S(1)} fusion(f32[64,24576]{1,0:T(8,128)S(1)} %fusion.50, f32[64,24576]{1,0:T(8,128)S(1)} %copy-done.2), kind=kOutput, calls=%fused_computation.29 | convolution fusion | flops 1207959552 | bytes 12599296 | tf_op jit(solution)/shard_map/dot_general | solution.py:21
  133.3 64.7 %psum.15 = f32[64,64]{0,1:T(8,128)S(1)} all-reduce(f32[64,64]{0,1:T(8,128)S(1)} %convolution_bitcast_fusion.4), channel_id=1, replica_groups=mesh['sector'=16,'slab'=8] {'sector','slab'}, use_global_device_ids=true, to_apply=%region_6.9 | all-reduce | flops 4096 | bytes 32768 | tf_op jit(solution)/shard_map/psum | solution.py:100
  198.2 5.8 %cholesky.55 = f32[64,64]{1,0:T(8,128)S(1)} custom-call(f32[64,64]{1,0:T(8,128)S(1)} %fusion.18), custom_call_target="Cholesky" | custom-call | tf_op jit(solution)/shard_map/jit(cholesky)/cholesky | solution.py:31
  205.4 4.9 custom-call.8
  212.3 128.1 %while.13 = (s32[]{:T(128)}, f32[64,64]{0,1:T(8,128)S(1)}, f32[64,64]{0,1:T(8,128)S(1)}, s32[]{:T(128)}, s32[]{:T(128)}) while((s32[]{:T(128)}, f32[64,64]{0,1:T(8,128)S(1)}, f32[64,64]{0,1:T(8,128)S(1)}, s32[]{:T(128)}, s32[]{:T(128)}) %tuple.51), condition=%wide.region_5.0_spmd, body=%wide.region_3.0_spmd.sunk | while | flops 196929 | bytes 85849 | solution.py:48
  341.0 5.3 %fusion.49 = f32[32,24576]{1,0:T(8,128)S(1)} fusion(f32[32,64]{1,0:T(8,128)S(1)} %fusion.48, f32[64,24576]{1,0:T(8,128)} %reshape.80), kind=kOutput, calls=%fused_computation.88 | convolution fusion | flops 603979776 | bytes 9445376 | tf_op jit(solution)/shard_map/dot_general | solution.py:21
  346.3 4.9 broadcast_multiply_fusion
  351.2 3.1 pad_maximum_fusion.2
  354.4 7.0 %reshape.84 = f32[64,8,12,256]{3,2,1,0:T(8,128)} reshape(f32[64,24576]{1,0:T(8,128)} %pad_maximum_fusion.2) | data formatting | bytes 12582912 | tf_op jit(solution)/shard_map/reshape | solution.py:109
  361.4 1.7 fusion.44
  363.1 1.3 copy.74
  364.5 1.3 copy.71
  365.8 4.0 collective-permute-start
  369.8 5.5 %fusion.46 = (f32[64,8,1,256]{3,2,1,0:T(1,128)}, f32[64,8,1,256]{3,2,1,0:T(1,128)}) fusion(f32[64,8,12,256]{3,2,1,0:T(8,128)} %reshape.84), kind=kLoop, calls=%fused_computation.85 | loop fusion | bytes 2097152 | tf_op jit(solution)/shard_map/slice | solution.py:13
  375.3 2.6 collective-permute-start.2
  377.9 5.7 %collective-permute-start.3 = (f32[64,8,1,256]{3,2,1,0:T(1,128)}, f32[64,8,1,256]{3,2,1,0:T(1,128)}, u32[]{:S(2)}, u32[]{:S(2)}) collective-permute-start(f32[64,8,1,256]{3,2,1,0:T(1,128)} %get-tuple-element.120), channel_id=1, source_target_pairs={{0,1},{1,2},{2,3},{3,4},{4,5},{5,6},{6,7},{8,9},{9,10},{10,11},{11... | collective-permute-start | bytes 1572872 | tf_op jit(solution)/shard_map/ppermute | solution.py:14
  383.6 12.2 %fusion.45 = (f32[64,7,12,256]{3,2,1,0:T(8,128)}, f32[64,7,12,256]{3,2,1,0:T(8,128)}) fusion(f32[64,8,12,256]{3,2,1,0:T(8,128)} %reshape.84), kind=kLoop, calls=%fused_computation.84 | loop fusion | bytes 22020096 | tf_op jit(solution)/shard_map/slice | solution.py:75
  396.0 2.5 reshape.81
  398.5 3.9 reshape.83
  402.4 6.9 %copy.78 = f32[32,8,12,256]{3,1,2,0:T(8,128)} copy(f32[32,8,12,256]{3,2,1,0:T(8,128)} %reshape.83) | data formatting | bytes 6291456
  409.2 4.5 copy.77
  414.7 3.6 copy.75
  418.3 3.7 gather_fusion.1
  421.9 3.2 select_bitcast_fusion
  425.2 3.9 copy.76
  429.1 3.6 copy.72
  432.7 3.7 gather_fusion
  436.4 3.2 select_bitcast_fusion.1
  439.6 3.8 copy.73
  443.4 23.0 %fusion.3 = f32[64,8,12,256]{3,2,1,0:T(8,128)S(1)} fusion(f32[64,8,12,256]{3,2,1,0:T(8,128)} %reshape.84, f32[64,8,1,256]{3,2,1,0:T(1,128)} %collective-permute-done.3, f32[64,8,1,256]{3,2,1,0:T(1,128)} %collective-permute-done.2, f32[64,1,12,256]{3,2,1,0:T(8,128)} %copy.73, f32[64,7,12,256]{3,2,1,0:T(8,128)} %get-tuple-element.118, ...), kind=kLoop, calls=%fused_computation.14 | loop fusion | flops 17301504 | bytes 26214400 | tf_op jit(solution)/shard_map/sub | solution.py:80
  466.5 4.2 fusion.43
  470.6 3.7 slice.67
  474.3 4.8 sub.45
  479.1 3.8 reshape.86
  482.9 6.7 %copy.80 = f32[32,8,12,256]{3,1,2,0:T(8,128)} copy(f32[32,8,12,256]{3,2,1,0:T(8,128)} %reshape.86) | data formatting | bytes 6291456
  489.6 3.7 slice.65
  493.3 3.9 multiply_subtract_fusion
  497.2 3.7 reshape.85
  501.0 6.7 %copy.79 = f32[32,8,12,256]{3,1,2,0:T(8,128)} copy(f32[32,8,12,256]{3,2,1,0:T(8,128)} %reshape.85) | data formatting | bytes 6291456
  (444 shorter events, 89.1 us)
Async XLA Ops:
  0.6 210.1 %copy-start = (f32[64,64]{1,0:T(8,128)S(1)}, f32[64,64]{1,0:T(8,128)}, u32[]{:S(2)}) copy-start(f32[64,64]{1,0:T(8,128)} %param.17) | copy-start | bytes 49156
  0.6 12.4 %copy-start.4 = (f32[64,8,12,256]{3,1,2,0:T(8,128)S(1)}, f32[64,8,12,256]{3,1,2,0:T(8,128)}, u32[]{:S(2)}) copy-start(f32[64,8,12,256]{3,1,2,0:T(8,128)} %param.14) | copy-start | bytes 18874372
  120.0 8.1 %copy-start.2 = (f32[64,24576]{1,0:T(8,128)S(1)}, f32[64,24576]{1,0:T(8,128)}, u32[]{:S(2)}) copy-start(f32[64,24576]{1,0:T(8,128)} %reshape.82) | copy-start | bytes 18874372
  128.1 83.7 %copy-start.8 = (s32[64]{0:T(128)S(1)}, s32[64]{0:T(128)}, u32[]{:S(2)}) copy-start(s32[64]{0:T(128)} %param.18) | copy-start | bytes 772
  128.1 212.3 %copy-start.9 = (s32[32]{0:T(128)S(1)}, s32[32]{0:T(128)}, u32[]{:S(2)}) copy-start(s32[32]{0:T(128)} %param.19) | copy-start | bytes 388
  128.1 212.8 %copy-start.6 = (f32[8,12,256]{2,0,1:T(8,128)S(1)}, f32[8,12,256]{2,0,1:T(8,128)}, u32[]{:S(2)}) copy-start(f32[8,12,256]{2,0,1:T(8,128)} %param.16) | copy-start | bytes 294916
  341.0 5.3 %copy-start.3 = (f32[64,24576]{1,0:T(8,128)S(1)}, f32[64,24576]{1,0:T(8,128)}, u32[]{:S(2)}) copy-start(f32[64,24576]{1,0:T(8,128)} %reshape.82) | copy-start | bytes 18874372
  364.5 50.2 %collective-permute-start.1 = (f32[64,1,12,256]{3,0,2,1:T(8,128)}, f32[64,1,12,256]{3,0,2,1:T(8,128)}, u32[]{:S(2)}, u32[]{:S(2)}) collective-permute-start(f32[64,1,12,256]{3,0,2,1:T(8,128)} %copy.74), channel_id=1, source_target_pairs={{0,8},{8,16},{16,24},{24,32},{32,40},{40,48},{48,56},{56,64},{64,7... | collective-permute-start | bytes 2359304 | tf_op jit(solution)/shard_map/ppermute | solution.py:14
  365.8 63.3 %collective-permute-start = (f32[64,1,12,256]{3,0,2,1:T(8,128)}, f32[64,1,12,256]{3,0,2,1:T(8,128)}, u32[]{:S(2)}, u32[]{:S(2)}) collective-permute-start(f32[64,1,12,256]{3,0,2,1:T(8,128)} %copy.71), channel_id=1, source_target_pairs={{8,0},{16,8},{24,16},{32,24},{40,32},{48,40},{56,48},{64,56},{72,6... | collective-permute-start | bytes 2359304 | tf_op jit(solution)/shard_map/ppermute | solution.py:15
  375.3 68.1 %collective-permute-start.2 = (f32[64,8,1,256]{3,2,1,0:T(1,128)}, f32[64,8,1,256]{3,2,1,0:T(1,128)}, u32[]{:S(2)}, u32[]{:S(2)}) collective-permute-start(f32[64,8,1,256]{3,2,1,0:T(1,128)} %get-tuple-element.119), channel_id=1, source_target_pairs={{1,0},{2,1},{3,2},{4,3},{5,4},{6,5},{7,6},{9,8},{10,9},{11,10},{12... | collective-permute-start | bytes 1572872 | tf_op jit(solution)/shard_map/ppermute | solution.py:15
  377.9 17.9 %copy-start.7 = (s32[256]{0:T(256)S(1)}, s32[256]{0:T(256)}, u32[]{:S(2)}) copy-start(s32[256]{0:T(256)} %param.20) | copy-start | bytes 3076
  377.9 65.5 %collective-permute-start.3 = (f32[64,8,1,256]{3,2,1,0:T(1,128)}, f32[64,8,1,256]{3,2,1,0:T(1,128)}, u32[]{:S(2)}, u32[]{:S(2)}) collective-permute-start(f32[64,8,1,256]{3,2,1,0:T(1,128)} %get-tuple-element.120), channel_id=1, source_target_pairs={{0,1},{1,2},{2,3},{3,4},{4,5},{5,6},{6,7},{8,9},{9,10},{10,11},{11... | collective-permute-start | bytes 1572872 | tf_op jit(solution)/shard_map/ppermute | solution.py:14
  402.4 6.9 %copy-start.5 = (f32[32,8,12,256]{3,2,1,0:T(8,128)S(1)}, f32[32,8,12,256]{3,2,1,0:T(8,128)}, u32[]{:S(2)}) copy-start(f32[32,8,12,256]{3,2,1,0:T(8,128)} %reshape.81) | copy-start | bytes 9437188
  493.3 14.4 %copy-start.1 = (f32[64,64]{1,0:T(8,128)S(1)}, f32[64,64]{1,0:T(8,128)}, u32[]{:S(2)}) copy-start(f32[64,64]{1,0:T(8,128)} %param.17) | copy-start | bytes 49156
where the time goes:
time: 514 us; the launch traced here: 508 us
  local copies, waits for them, and re-layouts  133 us (26%)
  blocking collectives  131 us (25%)
  matrix products  119 us (23%)
  other arithmetic  66 us (13%)
  loops' own time  45.8 us (9%)
  starting transfers between devices  12.3 us (2%)
    dot_general x271, matrix products, exact_dot(): jnp.dot(left_operator, right_operator, precision=lax.Precision.HIGHEST)  118 us
    psum x1, blocking collectives, local(): lax.psum(exact_dot(right_rows, right_rows.T), ('sector', 'slab'))  66 us
    psum x1, blocking collectives, local(): lax.psum(exact_dot(left_rows, normalized.T), ('sector', 'slab')) / row_total  64.7 us
    another operation x1, loops' own time, orthonormal(): lax.fori_loop(0, matrix.shape[1], column_step, jnp.zeros_like(matrix))  45.8 us
    unnamed x27, local copies, waits for them, and re-layouts  39.8 us
    sub x1, other arithmetic, laplace(): return final_result - padded[..., 2:] - padded[..., :-2]  23 us
    slice x1, local copies, waits for them, and re-layouts, laplace(): vector_columns[:, :-1]  12.2 us
  transfers between devices with their start and end apart: 4, of which 0 were waited for; matrix products, arithmetic and copies ran while one was open for 13% of the time, Pallas kernels for 0%

commit v1 on v0

--- a/solution.py
+++ b/solution.py
@@ -93,7 +93,10 @@
         jnp.where(rim_map[:, None] == places[None, :], places[:, None], 0), axis=0
     )
     row_total = right_rows.shape[1] * lax.axis_size("sector") * lax.axis_size("slab")
-    right_gram = lax.psum(exact_dot(right_rows, right_rows.T), ("sector", "slab")) / row_total
+    right_gram = (
+        jnp.sum(lax.all_gather(exact_dot(right_rows, right_rows.T), ("sector", "slab")), axis=0)
+        / row_total
+    )
     lower_factor = jnp.linalg.cholesky(right_gram)
     lower_inverse_mat = lower_inverse(lower_factor)
     normalized = exact_dot(lower_inverse_mat, right_rows)

time: 514 us -> 765 us (1.49)
  waiting for transfers between devices: 0.01 us -> 276 us
  blocking collectives: 131 us -> 65.6 us
  matrix products: 119 us -> 134 us
  between operations: 1.25 us -> 14.8 us
    all_gather x0 -> x1, waiting for transfers between devices: none -> 276 us  [local(): lax.all_gather(exact_dot(right_rows, right_rows.T), ('sector', 'slab'))]
    psum x1 -> x0, blocking collectives: 66 us -> none  [local(): lax.psum(exact_dot(right_rows, right_rows.T), ('sector', 'slab'))]
    dot_general x271, matrix products: 118 us -> 133 us  [exact_dot(): jnp.dot(left_operator, right_operator, precision=lax.Precision.HIGHEST)]
    unnamed x27 -> x25, local copies, waits for them, and re-layouts: 39.8 us -> 42.6 us
  transfers between devices with their start and end apart: 4 -> 5, of which waited for: 0 -> 1; matrix products, arithmetic and copies ran while one was open for 13% -> 11% of each run, Pallas kernels for 0% -> 0%
where the time goes in v1:
time: 765 us; the launch traced here: 753 us
  waiting for transfers between devices  276 us (36%)
  local copies, waits for them, and re-layouts  136 us (18%)
  matrix products  134 us (18%)
  other arithmetic  68.4 us (9%)
  blocking collectives  65.6 us (9%)
  loops' own time  45.8 us (6%)
  between operations  14.8 us (2%)
  starting transfers between devices  12.2 us (2%)
    all_gather x1, waiting for transfers between devices, local(): lax.all_gather(exact_dot(right_rows, right_rows.T), ('sector', 'slab'))  276 us
    dot_general x271, matrix products, exact_dot(): jnp.dot(left_operator, right_operator, precision=lax.Precision.HIGHEST)  133 us
    psum x1, blocking collectives, local(): lax.psum(exact_dot(left_rows, normalized.T), ('sector', 'slab')) / row_total  65.6 us
    another operation x1, loops' own time, orthonormal(): lax.fori_loop(0, matrix.shape[1], column_step, jnp.zeros_like(matrix))  45.8 us
    unnamed x25, local copies, waits for them, and re-layouts  42.6 us
    sub x1, other arithmetic, laplace(): return final_result - padded[..., 2:] - padded[..., :-2]  22.9 us
  transfers between devices with their start and end apart: 5, of which 1 were waited for; matrix products, arithmetic and copies ran while one was open for 11% of the time, Pallas kernels for 0%

profile of v1, /device:TPU:24, one launch (start us, length us, event | category | flops | bytes accessed | tf_op | source)
XLA Modules:
  0.0 752.8 jit_solution(9889265226784889349)
XLA Ops:
  7.2 26.2 %fusion.9 = f32[64,64]{1,0:T(8,128)} fusion(f32[64,8,12,256]{3,1,2,0:T(8,128)} %param.14), kind=kOutput, calls=%fused_computation.28 | convolution fusion | flops 1207959552 | bytes 6307840 | tf_op jit(solution)/shard_map/dot_general | solution.py:21
  33.4 8.9 %copy.65 = f32[64,8,12,256]{3,2,1,0:T(8,128)} copy(f32[64,8,12,256]{3,1,2,0:T(8,128)} %param.14) | data formatting | bytes 12582912 | tf_op args[0]
  42.3 6.8 reshape.80
  49.1 8.9 %copy.66 = f32[64,8,12,256]{3,2,1,0:T(8,128)} copy(f32[64,8,12,256]{3,1,2,0:T(8,128)} %param.15) | data formatting | bytes 12582912 | tf_op args[1]
  58.0 6.8 reshape.82
  65.0 276.3 %all-gather.3.cloned.1.call-done = f32[8192,64]{1,0:T(8,128)} async-done(((f32[64,64]{1,0:T(8,128)}), f32[8192,64]{1,0:T(8,128)}) %all-gather.3.cloned.1.call-update) | async-done | bytes 2097168 | tf_op jit(solution)/shard_map/all_gather | solution.py:97
  341.3 2.5 reduce_sum.31
  344.1 5.8 cholesky.44
  351.3 4.9 custom-call.10
  356.4 8.1 %fusion.50 = f32[64,24576]{1,0:T(8,128)S(1)} fusion(f32[64,64]{1,0:T(8,128)S(1)} %fusion.19, f32[64,24576]{1,0:T(8,128)} %reshape.80), kind=kOutput, calls=%fused_computation.89 | convolution fusion | flops 1207959552 | bytes 12599296 | tf_op jit(solution)/shard_map/dot_general | solution.py:21
  364.6 5.1 convolution_bitcast_fusion.4
  369.7 65.6 %psum.7 = f32[64,64]{0,1:T(8,128)S(1)} all-reduce(f32[64,64]{0,1:T(8,128)S(1)} %convolution_bitcast_fusion.4), channel_id=1, replica_groups=mesh['sector'=16,'slab'=8] {'sector','slab'}, use_global_device_ids=true, to_apply=%region_6.9 | all-reduce | flops 4096 | bytes 32768 | tf_op jit(solution)/shard_map/psum | solution.py:103
  435.6 5.8 cholesky.55
  442.8 4.9 custom-call.8
  449.7 128.1 %while.13 = (s32[]{:T(128)}, f32[64,64]{0,1:T(8,128)S(1)}, f32[64,64]{0,1:T(8,128)S(1)}, s32[]{:T(128)}, s32[]{:T(128)}) while((s32[]{:T(128)}, f32[64,64]{0,1:T(8,128)S(1)}, f32[64,64]{0,1:T(8,128)S(1)}, s32[]{:T(128)}, s32[]{:T(128)}) %tuple.51), condition=%wide.region_5.0_spmd, body=%wide.region_3.0_spmd.sunk | while | flops 196929 | bytes 85849 | solution.py:48
  578.3 5.1 fusion.49
  583.4 6.3 broadcast_multiply_fusion
  589.7 3.1 pad_maximum_fusion.2
  592.9 7.0 reshape.84
  599.9 12.2 %fusion.45 = (f32[64,7,12,256]{3,2,1,0:T(8,128)}, f32[64,7,12,256]{3,2,1,0:T(8,128)}) fusion(f32[64,8,12,256]{3,2,1,0:T(8,128)} %reshape.84), kind=kLoop, calls=%fused_computation.84 | loop fusion | bytes 22020096 | tf_op jit(solution)/shard_map/slice | solution.py:75
  612.0 1.7 fusion.44
  615.1 1.4 copy.69
  616.4 4.0 collective-permute-start
  620.5 5.5 fusion.46
  626.0 2.4 reshape.81
  628.4 4.1 collective-permute-start.2
  632.4 4.1 collective-permute-start.3
  636.5 3.9 reshape.83
  640.4 6.9 copy.76
  647.3 4.5 copy.75
  652.7 3.6 copy.73
  656.3 3.7 gather_fusion.1
  660.0 3.2 select_bitcast_fusion
  663.3 3.9 copy.74
  667.1 3.6 copy.70
  670.7 3.7 gather_fusion
  674.4 3.2 select_bitcast_fusion.1
  677.6 3.8 copy.71
  681.4 22.9 %fusion.3 = f32[64,8,12,256]{3,2,1,0:T(8,128)S(1)} fusion(f32[64,8,12,256]{3,2,1,0:T(8,128)} %reshape.84, f32[64,8,1,256]{3,2,1,0:T(1,128)} %collective-permute-done.3, f32[64,8,1,256]{3,2,1,0:T(1,128)} %collective-permute-done.2, f32[64,1,12,256]{3,2,1,0:T(8,128)} %copy.71, f32[64,7,12,256]{3,2,1,0:T(8,128)} %get-tuple-element.118, ...), kind=kLoop, calls=%fused_computation.14 | loop fusion | flops 17301504 | bytes 26214400 | tf_op jit(solution)/shard_map/sub | solution.py:80
  704.3 4.2 fusion.43
  708.5 3.7 slice.67
  712.2 4.8 sub.45
  717.0 3.8 reshape.86
  720.8 6.7 copy.78
  727.5 3.7 slice.65
  731.2 3.9 multiply_subtract_fusion
  735.1 3.7 reshape.85
  738.9 6.7 copy.77
  (447 shorter events, 90.6 us)
Async XLA Ops:
  7.2 441.0 %copy-start = (f32[64,64]{1,0:T(8,128)S(1)}, f32[64,64]{1,0:T(8,128)}, u32[]{:S(2)}) copy-start(f32[64,64]{1,0:T(8,128)} %param.17) | copy-start | bytes 49156
  7.2 334.2 %all-gather.3.cloned.1.call-start = ((), (), s32[]{:S(2)}) async-start(), calls=%async_computation | async-start | bytes 4227072 | tf_op jit(solution)/shard_map/all_gather | solution.py:97
  57.9 6.8 copy-start.3
  58.0 6.9 copy-start.4
  344.0 20.5 %slice-start = ((s8[6291456]{0:T(1024)(128)(4,1)}), s8[2097152]{0:T(1024)(128)(4,1)S(1)}, s32[]{:S(2)}) async-start(s8[6291456]{0:T(1024)(128)(4,1)} %bitcast.110), calls=%async_computation.1 | async-start | bytes 4194304
  356.4 8.1 %slice-start.1 = ((s8[6291456]{0:T(1024)(128)(4,1)}), s8[4194304]{0:T(1024)(128)(4,1)S(1)}, s32[]{:S(2)}) async-start(s8[6291456]{0:T(1024)(128)(4,1)} %bitcast.110), calls=%async_computation.2 | async-start | bytes 8388608
  364.6 84.7 %copy-start.5 = (s32[64]{0:T(128)S(1)}, s32[64]{0:T(128)}, u32[]{:S(2)}) copy-start(s32[64]{0:T(128)} %param.18) | copy-start | bytes 772
  364.6 213.2 %copy-start.6 = (s32[32]{0:T(128)S(1)}, s32[32]{0:T(128)}, u32[]{:S(2)}) copy-start(s32[32]{0:T(128)} %param.19) | copy-start | bytes 388
  615.1 37.6 %collective-permute-start.1 = (f32[64,1,12,256]{3,0,2,1:T(8,128)}, f32[64,1,12,256]{3,0,2,1:T(8,128)}, u32[]{:S(2)}, u32[]{:S(2)}) collective-permute-start(f32[64,1,12,256]{3,0,2,1:T(8,128)} %copy.72), channel_id=1, source_target_pairs={{0,8},{8,16},{16,24},{24,32},{32,40},{40,48},{48,56},{56,64},{64,7... | collective-permute-start | bytes 2359304 | tf_op jit(solution)/shard_map/ppermute | solution.py:14
  616.4 50.7 %collective-permute-start = (f32[64,1,12,256]{3,0,2,1:T(8,128)}, f32[64,1,12,256]{3,0,2,1:T(8,128)}, u32[]{:S(2)}, u32[]{:S(2)}) collective-permute-start(f32[64,1,12,256]{3,0,2,1:T(8,128)} %copy.69), channel_id=1, source_target_pairs={{8,0},{16,8},{24,16},{32,24},{40,32},{48,40},{56,48},{64,56},{72,6... | collective-permute-start | bytes 2359304 | tf_op jit(solution)/shard_map/ppermute | solution.py:15
  628.4 53.0 %collective-permute-start.2 = (f32[64,8,1,256]{3,2,1,0:T(1,128)}, f32[64,8,1,256]{3,2,1,0:T(1,128)}, u32[]{:S(2)}, u32[]{:S(2)}) collective-permute-start(f32[64,8,1,256]{3,2,1,0:T(1,128)} %get-tuple-element.119), channel_id=1, source_target_pairs={{1,0},{2,1},{3,2},{4,3},{5,4},{6,5},{7,6},{9,8},{10,9},{11,10},{12... | collective-permute-start | bytes 1572872 | tf_op jit(solution)/shard_map/ppermute | solution.py:15
  632.4 49.0 %collective-permute-start.3 = (f32[64,8,1,256]{3,2,1,0:T(1,128)}, f32[64,8,1,256]{3,2,1,0:T(1,128)}, u32[]{:S(2)}, u32[]{:S(2)}) collective-permute-start(f32[64,8,1,256]{3,2,1,0:T(1,128)} %get-tuple-element.120), channel_id=1, source_target_pairs={{0,1},{1,2},{2,3},{3,4},{4,5},{5,6},{6,7},{8,9},{9,10},{10,11},{11... | collective-permute-start | bytes 1572872 | tf_op jit(solution)/shard_map/ppermute | solution.py:14
  640.4 6.9 copy-start.2
  731.2 14.4 %copy-start.1 = (f32[64,64]{1,0:T(8,128)S(1)}, f32[64,64]{1,0:T(8,128)}, u32[]{:S(2)}) copy-start(f32[64,64]{1,0:T(8,128)} %param.17) | copy-start | bytes 49156
Sparse Core Ops, SparseCore 0:
  33.5 307.7 all-gather.2
